TPU v7x, 32 devices: a whole 2x2x4 slice. The times are simulated.
32 devices in a mesh: series: 4 (over y, x), tm: 8 (over z, core).
Axes of the slice: x: 2, y: 2, z: 4, core: 2. Of those that a mesh axis runs over, the one named last changes fastest.
Arguments:
- observed: bfloat16 [5120, 6144], P('series', 'tm'), may hold values from -6 to 6
- mask: int32 [5120, 6144], P('series', 'tm'), may hold values 0 or 1
- series_factors: float32 [5120, 256], P('series'), may hold values from -6 to 6
- time_factors: float32 [256, 6144], P(None, 'tm'), may hold values from -0.375 to 0.375
- ar_weights: float32 [3, 256], replicated, may hold values from -0.7 to 0.7
Outputs:
- series_out: float32 [5120, 256], P('series')
- time_out: float32 [256, 6144], P(None, 'tm')
- imputed: bfloat16 [5120, 6144], P('series', 'tm')
Inputs may be any that keep to these rules, and one draw needn't show every extreme that they name: mask holds only 0 and 1.
All inputs are finite; a program needn't handle non-finite values. No bound on the sum of `mask` on one device may be relied on, other than what follows from the above.
Results may differ from a plain program's by a relative error of at most 0.0089.
Values sent between devices are 32-bit elements; how exact they have to be, the bound alone decides.
A program may use at most 128 MiB of HBM per device.

v0:
```python
import functools

import jax
import jax.numpy as jnp
from jax import lax
from jax.experimental import pallas as pl
from jax.experimental.pallas import tpu as pltpu
from jax.sharding import PartitionSpec as P

ITERS = 2
LAGS = (1, 24, 168)
HALO = 256
HALF = 64
BLOCK = 2 * HALF
WIDE = 2
TAIL_STEPS = 2
PARTS = 2
LAG_STEPS = 4
EARLY = 0
G_STEPS = ((5, 7), (5, 7))


def kernel(
    series_size, tm_size,
    obs_hbm, mask_hbm, f_hbm, x_hbm, w_in,
    f_out, x_out,
    obs, mask, f_in, x_in, ar, f_new, x_new, misfit, f_low, x_low, grad, partner_in, left_in, right_in,
    g_loc, g_in, halo_l, halo_r, w_cols,
    load_sem, first_sem, out_sem, pair_send, pair_recv, line_send, left_recv, right_recv,
    out_send, gather_recv, give_send, give_recv, g_send, g_recv, x_send, x_recv,
    edge_send, edge_recv,
):
    rows, rank = f_in.shape
    hours = x_in.shape[1]
    blocks = rows // BLOCK
    piece = rank // series_size
    hours_all = hours * tm_size
    sensors_all = rows * series_size
    step_f = rank / hours_all
    step_x = 1.0 / sensors_all
    ridge_f = 0.1 * hours_all / rank
    ridge_x = 0.1 * sensors_all
    lam_ar = sensors_all / 8.0

    s = lax.axis_index("series")
    tm = lax.axis_index("tm")
    chips = tm_size // 2
    chip, core = tm // 2, tm % 2
    other = 1 - core
    owner = chips // 2 - 1 + core
    partner = chip * 2 + other
    is_owner = chip == owner
    before = chip < owner
    after = chip > owner
    has_left = chip > 0
    has_right = chip < chips - 1
    at_end = jnp.logical_or(jnp.logical_and(before, chip == 0), jnp.logical_and(after, chip == chips - 1))
    relay = jnp.logical_and(jnp.logical_not(is_owner), jnp.logical_not(at_end))

    def both(a, b):
        return jnp.logical_and(a, b)

    def remote(src, dst, ssem, rsem, series_to, tm_to):
        return pltpu.make_async_remote_copy(
            src_ref=src, dst_ref=dst, send_sem=ssem, recv_sem=rsem,
            device_id=(series_to, tm_to), device_id_type=pl.DeviceIdType.MESH,
        )

    def block_rows(b):
        return pl.ds(pl.multiple_of(b * BLOCK, BLOCK), BLOCK)

    def half_rows(b, which):
        return pl.ds(pl.multiple_of(b * BLOCK + which * HALF, HALF), HALF)

    def slot_rows(b):
        return pl.ds(pl.multiple_of(b * HALF, HALF), HALF)

    def piece_rows(i):
        return pl.ds(pl.multiple_of(i * piece, piece), piece)

    def load_copies(b):
        return (
            pltpu.make_async_copy(obs_hbm.at[block_rows(b), :], obs.at[block_rows(b), :], load_sem.at[0, b]),
            pltpu.make_async_copy(mask_hbm.at[block_rows(b), :], mask.at[block_rows(b), :], load_sem.at[1, b]),
        )

    f_load = pltpu.make_async_copy(f_hbm, f_in, first_sem.at[0])
    x_load = pltpu.make_async_copy(x_hbm, x_in, first_sem.at[1])
    x_load.start()
    f_load.start()

    @pl.loop(0, blocks)
    def _(b):
        for c in load_copies(b):
            c.start()

    for lag in range(3):
        w_cols[lag] = jnp.transpose(jnp.broadcast_to(w_in[lag : lag + 1, :], (128, rank)))
    x_load.wait()

    barrier = pltpu.get_barrier_semaphore()
    for d in (-2, -1, 1, 2):
        @pl.when(both(tm + d >= 0, tm + d < tm_size))
        def _():
            pl.semaphore_signal(barrier, inc=1, device_id=(s, tm + d), device_id_type=pl.DeviceIdType.MESH)
    for d in range(1, series_size):
        pl.semaphore_signal(
            barrier, inc=1, device_id=(lax.rem(s + d, series_size), tm), device_id_type=pl.DeviceIdType.MESH
        )
    pl.semaphore_wait(barrier, series_size - 1 + jnp.minimum(tm, 2) + jnp.minimum(tm_size - 1 - tm, 2))

    def edge_copies(it, source):
        to_right = remote(
            source.at[piece_rows(s), pl.ds(hours - HALO, HALO)], halo_l.at[it],
            edge_send.at[it, 0], edge_recv.at[it, 0], s, tm + 1,
        )
        to_left = remote(
            source.at[piece_rows(s), pl.ds(0, HALO)], halo_r.at[it],
            edge_send.at[it, 1], edge_recv.at[it, 1], s, tm - 1,
        )
        return to_right, to_left

    def start_edges(it, source):
        to_right, to_left = edge_copies(it, source)
        pl.when(tm < tm_size - 1)(to_right.start)
        pl.when(tm > 0)(to_left.start)

    start_edges(0, x_in)
    f_load.wait()

    spread_done = blocks + EARLY - LAG_STEPS
    earlier_spread = None
    for it in range(ITERS):
        f_now = f_in if it == 0 else f_new.at[it - 1]
        x_now = x_in if it == 0 else x_new.at[it - 1]

        def pair_copy(b, it=it):
            return remote(
                grad.at[it, half_rows(b, other), :], partner_in.at[it, slot_rows(b), :],
                pair_send.at[it, b], pair_recv.at[it, b], s, partner,
            )

        def to_right_copy(b, it=it):
            return remote(
                grad.at[it, half_rows(b, core), :], left_in.at[it, slot_rows(b), :],
                line_send.at[it, b], left_recv.at[it, b], s, tm + 2,
            )

        def to_left_copy(b, it=it):
            return remote(
                grad.at[it, half_rows(b, core), :], right_in.at[it, slot_rows(b), :],
                line_send.at[it, b], right_recv.at[it, b], s, tm - 2,
            )

        def spread_copies(b, it=it):
            rows_own = half_rows(b, core)
            view = f_new.at[it, rows_own, :]
            left = remote(view, view, out_send.at[it, 0, b], gather_recv.at[it, b], s, tm - 2)
            right = remote(view, view, out_send.at[it, 1, b], gather_recv.at[it, b], s, tm + 2)
            give = remote(view, view, give_send.at[it, b], give_recv.at[it, b], s, partner)
            return left, right, give

        def give_wait(b, it=it):
            view = f_new.at[it, half_rows(b, other), :]
            remote(view, view, give_send.at[it, b], give_recv.at[it, b], s, partner).wait_recv()

        def send_inward(b):
            pl.when(before)(to_right_copy(b).start)
            pl.when(after)(to_left_copy(b).start)

        def merge(b):
            pair_copy(b).wait_recv()
            grad[it, half_rows(b, core), :] += partner_in[it, slot_rows(b), :]
            pl.when(at_end)(lambda: send_inward(b))

        x_low[...] = x_now[...].astype(jnp.bfloat16)

        def wide_rows(w):
            return pl.ds(pl.multiple_of(w * WIDE * BLOCK, WIDE * BLOCK), WIDE * BLOCK)

        def row_pass(w, carry, earlier_spread=earlier_spread):
            for part in range(WIDE):
                here = w * WIDE + part
                if it == 0:
                    for c in load_copies(here):
                        c.wait()
                else:
                    pl.when(here >= spread_done)(lambda: earlier_spread(here))
            if it > 0:
                for part in range(WIDE):
                    give_wait(w * WIDE + part, it - 1)
            span = wide_rows(w)
            low = f_now[span, :].astype(jnp.bfloat16)
            f_low[span, :] = low
            product = jnp.dot(low, x_low[...], preferred_element_type=jnp.float32)
            miss = jnp.where(
                mask[span, :] != 0,
                product - obs[span, :].astype(jnp.float32),
                jnp.zeros_like(product),
            ).astype(jnp.bfloat16)
            misfit[span, :] = miss
            grad[it, span, :] = lax.dot_general(
                miss, x_low[...], (((1,), (1,)), ((), ())), preferred_element_type=jnp.float32
            )
            for part in range(WIDE):
                pair_copy(w * WIDE + part).start()

            @pl.when(w > 0)
            def _():
                for part in range(WIDE):
                    merge((w - 1) * WIDE + part)

            return carry

        def columns(part):
            return pl.ds(part * (hours // PARTS), hours // PARTS)

        def g_copy(d, part, it=it):
            to = lax.rem(s + d, series_size)
            return remote(
                g_loc.at[it, piece_rows(to), columns(part)], g_in.at[it, d - 1, :, columns(part)],
                g_send.at[it, part, d - 1], g_recv.at[it, part, d - 1], to, tm,
            )

        def x_copy(d, part, it=it):
            to = lax.rem(s + d, series_size)
            view = x_new.at[it, piece_rows(s), columns(part)]
            return remote(view, view, x_send.at[it, part, d - 1], x_recv.at[it, part, d - 1], to, tm)

        def x_wait(d, part, it=it):
            source = lax.rem(s + series_size - d, series_size)
            view = x_new.at[it, piece_rows(source), columns(part)]
            remote(view, view, x_send.at[it, part, d - 1], x_recv.at[it, part, d - 1], s, tm).wait_recv()

        wide = blocks // WIDE
        lax.fori_loop(0, wide, row_pass, 0)
        for part in range(WIDE):
            merge((wide - 1) * WIDE + part)
        for part in range(PARTS):
            g_loc[it, :, columns(part)] = lax.dot_general(
                f_low[...], misfit[:, columns(part)], (((0,), (0,)), ((), ())),
                preferred_element_type=jnp.float32,
            )
            for d in range(1, series_size):
                g_copy(d, part).start()
        def relay_step(b):
            @pl.when(both(relay, before))
            def _():
                to_right_copy(b).wait_recv()
                grad[it, half_rows(b, core), :] += left_in[it, slot_rows(b), :]
                to_right_copy(b).start()

            @pl.when(both(relay, after))
            def _():
                to_left_copy(b).wait_recv()
                grad[it, half_rows(b, core), :] += right_in[it, slot_rows(b), :]
                to_left_copy(b).start()

            @pl.when(is_owner)
            def _():
                @pl.when(has_left)
                def _():
                    to_right_copy(b).wait_recv()
                    grad[it, half_rows(b, core), :] += left_in[it, slot_rows(b), :]

                @pl.when(has_right)
                def _():
                    to_left_copy(b).wait_recv()
                    grad[it, half_rows(b, core), :] += right_in[it, slot_rows(b), :]

                old = f_now[half_rows(b, core), :]
                f_new[it, half_rows(b, core), :] = old - step_f * (grad[it, half_rows(b, core), :] + ridge_f * old)
                left, right, give = spread_copies(b)
                pl.when(has_left)(left.start)
                pl.when(has_right)(right.start)
                give.start()

        def spread_step(b, spread_copies=spread_copies):
            left, right, give = spread_copies(b)

            @pl.when(jnp.logical_not(is_owner))
            def _():
                left.wait_recv()
                pl.when(both(before, has_left))(left.start)
                pl.when(both(after, has_right))(right.start)
                give.start()

        def line_step(j, carry):
            pl.when(j < blocks)(lambda: relay_step(j))
            pl.when(j >= LAG_STEPS)(lambda: spread_step(j - LAG_STEPS))
            return carry

        to_right, to_left = edge_copies(it, x_now)

        @pl.when(tm > 0)
        def _():
            to_right.wait_recv()

        @pl.when(tm == 0)
        def _():
            halo_l[it] = jnp.zeros_like(halo_l[it])

        @pl.when(tm < tm_size - 1)
        def _():
            to_left.wait_recv()

        @pl.when(tm == tm_size - 1)
        def _():
            halo_r[it] = jnp.zeros_like(halo_r[it])

        own = x_now[piece_rows(s), :]
        extended = jnp.concatenate([halo_l[it], own, halo_r[it]], axis=1)
        width = hours + 2 * HALO
        weights = [w_cols[lag, piece_rows(s), :][:, 0:1] for lag in range(3)]
        resid = extended
        for lag in range(3):
            resid = resid - weights[lag] * pltpu.roll(extended, LAGS[lag], 1)
        hour = lax.broadcasted_iota(jnp.int32, (piece, width), 1) + (tm * hours - HALO)
        resid = jnp.where(both(hour >= 168, hour < hours_all), resid, jnp.zeros_like(resid))
        back = None
        for lag in range(3):
            term = weights[lag] * pltpu.roll(resid, width - LAGS[lag], 1)
            back = term if back is None else back + term
        ar[...] = (resid - back)[:, HALO : HALO + hours]

        done = 0
        for part in range(PARTS):
            lax.fori_loop(done, G_STEPS[it][part], line_step, 0)
            done = G_STEPS[it][part]
            total = g_loc[it, piece_rows(s), columns(part)]
            for d in range(1, series_size):
                g_copy(d, part).wait_recv()
                total = total + g_in[it, d - 1, :, columns(part)]
            old = x_now[piece_rows(s), columns(part)]
            x_new[it, piece_rows(s), columns(part)] = old - step_x * (
                total + ridge_x * old + lam_ar * ar[:, columns(part)]
            )
            for d in range(1, series_size):
                x_copy(d, part).start()
        if it < ITERS - 1:
            start_edges(it + 1, x_new.at[it])

        lax.fori_loop(done, blocks + (LAG_STEPS if it == ITERS - 1 else EARLY), line_step, 0)
        earlier_spread = spread_step
        for part in range(PARTS):
            for d in range(1, series_size):
                x_wait(d, part)

    last = ITERS - 1

    def f_store(b):
        return pltpu.make_async_copy(f_new.at[last, block_rows(b), :], f_out.at[block_rows(b), :], out_sem.at[b])

    x_store = pltpu.make_async_copy(x_new.at[last], x_out, out_sem.at[blocks])
    x_store.start()

    @pl.loop(0, blocks)
    def _(b):
        give_wait(b, last)
        f_store(b).start()

    for it in range(ITERS):
        to_right, to_left = edge_copies(it, x_in if it == 0 else x_new.at[it - 1])
        pl.when(tm < tm_size - 1)(to_right.wait_send)
        pl.when(tm > 0)(to_left.wait_send)
        for d in range(1, series_size):
            to = lax.rem(s + d, series_size)
            for part in range(PARTS):
                span = pl.ds(part * (hours // PARTS), hours // PARTS)
                remote(
                    g_loc.at[it, piece_rows(to), span], g_in.at[it, d - 1, :, span],
                    g_send.at[it, part, d - 1], g_recv.at[it, part, d - 1], to, tm,
                ).wait_send()
                view = x_new.at[it, piece_rows(s), span]
                remote(view, view, x_send.at[it, part, d - 1], x_recv.at[it, part, d - 1], to, tm).wait_send()

        @pl.loop(0, blocks)
        def _(b):
            line = grad.at[it, half_rows(b, core), :]
            view = f_new.at[it, half_rows(b, core), :]
            remote(
                grad.at[it, half_rows(b, other), :], partner_in.at[it, slot_rows(b), :],
                pair_send.at[it, b], pair_recv.at[it, b], s, partner,
            ).wait_send()

            @pl.when(jnp.logical_not(is_owner))
            def _():
                remote(line, left_in.at[it, slot_rows(b), :], line_send.at[it, b], left_recv.at[it, b], s, tm).wait_send()

            @pl.when(both(has_left, chip <= owner))
            def _():
                remote(view, view, out_send.at[it, 0, b], gather_recv.at[it, b], s, tm).wait_send()

            @pl.when(both(has_right, chip >= owner))
            def _():
                remote(view, view, out_send.at[it, 1, b], gather_recv.at[it, b], s, tm).wait_send()

            remote(view, view, give_send.at[it, b], give_recv.at[it, b], s, partner).wait_send()

    x_store.wait()

    @pl.loop(0, blocks)
    def _(b):
        f_store(b).wait()


def final_product(f_ref, x_ref, f_out, x_out, imputed, x_low):
    @pl.when(pl.program_id(0) == 0)
    def _():
        x_out[...] = x_ref[...]
        x_low[...] = x_ref[...].astype(jnp.bfloat16)

    f_out[...] = f_ref[...]
    imputed[...] = jnp.dot(
        f_ref[...].astype(jnp.bfloat16), x_low[...], preferred_element_type=jnp.float32
    ).astype(jnp.bfloat16)


def solution(mesh):
    series_size, tm_size = mesh.shape["series"], mesh.shape["tm"]

    def local(observed, mask, series_factors, time_factors, ar_weights):
        rows, rank = series_factors.shape
        hours = time_factors.shape[1]
        blocks = rows // BLOCK
        piece = rank // series_size
        peers = max(series_size - 1, 1)
        f32, bf16 = jnp.float32, jnp.bfloat16
        vmem = pl.BlockSpec(memory_space=pltpu.VMEM)
        anywhere = pl.BlockSpec(memory_space=pl.ANY)
        dma = pltpu.SemaphoreType.DMA
        half = (ITERS, rows // 2, rank)
        f_last, x_last = pl.pallas_call(
            functools.partial(kernel, series_size, tm_size),
            out_shape=(
                jax.ShapeDtypeStruct((rows, rank), f32),
                jax.ShapeDtypeStruct((rank, hours), f32),
            ),
            in_specs=[anywhere, anywhere, anywhere, anywhere, vmem],
            out_specs=(anywhere, anywhere),
            scratch_shapes=[
                pltpu.VMEM((rows, hours), bf16),
                pltpu.VMEM((rows, hours), jnp.int32),
                pltpu.VMEM((rows, rank), f32),
                pltpu.VMEM((rank, hours), f32),
                pltpu.VMEM((piece, hours), f32),
                pltpu.VMEM((ITERS, rows, rank), f32),
                pltpu.VMEM((ITERS, rank, hours), f32),
                pltpu.VMEM((rows, hours), bf16),
                pltpu.VMEM((rows, rank), bf16),
                pltpu.VMEM((rank, hours), bf16),
                pltpu.VMEM((ITERS, rows, rank), f32),
                pltpu.VMEM(half, f32),
                pltpu.VMEM(half, f32),
                pltpu.VMEM(half, f32),
                pltpu.VMEM((ITERS, rank, hours), f32),
                pltpu.VMEM((ITERS, peers, piece, hours), f32),
                pltpu.VMEM((ITERS, piece, HALO), f32),
                pltpu.VMEM((ITERS, piece, HALO), f32),
                pltpu.VMEM((3, rank, 128), f32),
                dma((2, blocks)),
                dma((2,)),
                dma((blocks + 1,)),
                dma((ITERS, blocks)), dma((ITERS, blocks)),
                dma((ITERS, blocks)), dma((ITERS, blocks)), dma((ITERS, blocks)),
                dma((ITERS, 2, blocks)), dma((ITERS, blocks)),
                dma((ITERS, blocks)), dma((ITERS, blocks)),
                dma((ITERS, PARTS, peers)), dma((ITERS, PARTS, peers)),
                dma((ITERS, PARTS, peers)), dma((ITERS, PARTS, peers)),
                dma((ITERS, 2)), dma((ITERS, 2)),
            ],
            compiler_params=pltpu.CompilerParams(
                collective_id=0, has_side_effects=True, vmem_limit_bytes=60 * 1024 * 1024
            ),
        )(observed, mask, series_factors, time_factors, ar_weights)
        tall = rows // TAIL_STEPS
        by_row = lambda width: pl.BlockSpec((tall, width), lambda i: (i, 0))
        whole = pl.BlockSpec((rank, hours), lambda i: (0, 0))
        return tuple(pl.pallas_call(
            final_product,
            grid=(TAIL_STEPS,),
            out_shape=(
                jax.ShapeDtypeStruct((rows, rank), f32),
                jax.ShapeDtypeStruct((rank, hours), f32),
                jax.ShapeDtypeStruct((rows, hours), bf16),
            ),
            in_specs=[by_row(rank), whole],
            out_specs=(by_row(rank), whole, by_row(hours)),
            scratch_shapes=[pltpu.VMEM((rank, hours), bf16)],
        )(f_last, x_last))

    in_specs = (P("series", "tm"), P("series", "tm"), P("series", None), P(None, "tm"), P())
    out_specs = (P("series", None), P(None, "tm"), P("series", "tm"))
    return jax.shard_map(local, mesh=mesh, in_specs=in_specs, out_specs=out_specs, check_vma=False)
```

profile of v0, /device:TPU:0, one launch (start us, length us, event | category | flops | bytes accessed | tf_op | source)
XLA Modules:
  0.0 68.1 jit_solution(781288708208261077)
XLA Ops:
  0.6 63.6 %shard_map.76 = (f32[1280,256]{1,0:T(8,128)}, f32[256,768]{1,0:T(8,128)}) custom-call(bf16[1280,768]{1,0:T(8,128)(2,1)} %obs_hbm.1, s32[1280,768]{1,0:T(8,128)} %mask_hbm.1, f32[1280,256]{1,0:T(8,128)} %f_hbm.1, f32[256,768]{1,0:T(8,128)} %x_hbm.1, f32[3,256]{1,0:T(4,128)} %w_in.1), custom_call_target="tpu_custom_call" | custom-call | tf_op jit(solution)/shard_map/pallas_call | solution.py:433
  64.3 3.8 %shard_map.77 = (f32[1280,256]{1,0:T(8,128)}, f32[256,768]{1,0:T(8,128)}, bf16[1280,768]{1,0:T(8,128)(2,1)}) custom-call(f32[1280,256]{1,0:T(8,128)} %get-tuple-element.5.f_ref, f32[256,768]{1,0:T(8,128)} %get-tuple-element.6.x_ref), custom_call_target="tpu_custom_call" | custom-call | tf_op jit(solution)/shard_map/pallas_call | solution.py:479
where the time goes:
time: 68.3 us; the launch traced here: 68.1 us
  Pallas kernels  67.4 us (99%)
    pallas_call x1, Pallas kernels, local(): pl.pallas_call(functools.partial(kernel, series_size, tm_size), out_shape...  63.6 us
    pallas_call x1, Pallas kernels, local(): pl.pallas_call(final_product, grid=(TAIL_STEPS,), out_shape=(jax.ShapeDty...  3.78 us

commit v1 on v0

v1 whole, which is shorter than its diff:
```python
import functools

import jax
import jax.numpy as jnp
from jax import lax
from jax.experimental import pallas as pl
from jax.experimental.pallas import tpu as pltpu
from jax.sharding import PartitionSpec as P

ITERS = 2
LAGS = (1, 24, 168)
HALO = 256
GROUP = 256
SUBS = 4
WIDTH = 256
LAG = 4
HOP = 3
TAIL_STEPS = 5
VMEM_BYTES = 67043328
VMEM_SPARE = 64 * 1024
Z_AT_G = ((1, 2, 3), (5, 6, 7))
Z_AT_AR = (5, 8)
Z_AT_X = (5, 8)
Z_PER_X = 2
Z_NEXT = (0, 0, 0, 2, 4)


def kernel(
    series_size, tm_size,
    obs_hbm, mask_hbm, f_hbm, x_hbm, w_in,
    f_out, x_out,
    obs, mask, f_in, x_in, f_mid, x_mid, ar, misfit, f_low, x_low, grad, partner_in, outer_in, inner_in,
    g_loc, up_in, cross_in, halo_l, halo_r, w_cols,
    load_sem, x_sem, pair_send, in_send, spread_send, give_send, up_send, cross_send, share_send, edge_send,
    pair_recv, give_recv, outer_recv, inner_recv, up_recv, cross_recv, share_recv, edge_recv,
):
    rows, rank = f_in.shape
    hours = x_in.shape[1]
    groups = rows // GROUP
    own = GROUP // 2
    sub = own // SUBS
    blocks = groups * SUBS
    parts = hours // WIDTH
    piece = rank // series_size
    hours_all = hours * tm_size
    sensors_all = rows * series_size
    step_f = rank / hours_all
    step_x = 1.0 / sensors_all
    ridge_f = 0.1 * hours_all / rank
    ridge_x = 0.1 * sensors_all
    lam_ar = sensors_all / 8.0

    s = lax.axis_index("series")
    tm = lax.axis_index("tm")
    core = tm % 2
    chip = tm // 2
    chips = tm_size // 2
    middle = chips // 2
    right = chip // middle
    toward = 1 - 2 * right
    distance = right * (chip - middle) + (1 - right) * (middle - 1 - chip)
    is_mid = distance == 0
    is_end = distance == middle - 1
    not_end = distance < middle - 1
    lag = LAG + HOP * distance
    last_lag = LAG + HOP * (middle - 1)
    partner = chip * 2 + (1 - core)
    inward = tm + 2 * toward
    outward = tm - 2 * toward

    half = series_size // 2
    high, low_bit = s // 2, s % 2
    place = (1 - low_bit) * high + low_bit * (series_size - 1 - high)

    def device_at(p):
        p = lax.rem(p + series_size, series_size)
        far = p // half
        return (1 - far) * 2 * p + far * (2 * (series_size - 1 - p) + 1)

    following, previous = device_at(place + 1), device_at(place - 1)

    def both(a, b):
        return jnp.logical_and(a, b)

    def remote(src, dst, ssem, rsem, series_to, tm_to):
        return pltpu.make_async_remote_copy(
            src_ref=src, dst_ref=dst, send_sem=ssem, recv_sem=rsem,
            device_id=(series_to, tm_to), device_id_type=pl.DeviceIdType.MESH,
        )

    def group_rows(g):
        return pl.ds(pl.multiple_of(g * GROUP, GROUP), GROUP)

    def own_rows(g, which):
        return pl.ds(pl.multiple_of(g * GROUP + which * own, own), own)

    def slot_group(g):
        return pl.ds(pl.multiple_of(g * own, own), own)

    def line_rows(j):
        return pl.ds(pl.multiple_of((j // SUBS) * GROUP + core * own + (j % SUBS) * sub, sub), sub)

    def slot_rows(j):
        return pl.ds(pl.multiple_of(j * sub, sub), sub)

    def piece_of(p):
        return lax.rem(place + series_size - p, series_size)

    def piece_rows(p):
        return pl.ds(pl.multiple_of(piece_of(p) * piece, piece), piece)

    def columns(c):
        return pl.ds(c * WIDTH, WIDTH)

    def load_copies(g):
        span = group_rows(g)
        return (
            pltpu.make_async_copy(f_hbm.at[span, :], f_in.at[span, :], load_sem.at[0, g]),
            pltpu.make_async_copy(mask_hbm.at[span, :], mask.at[span, :], load_sem.at[1, g]),
            pltpu.make_async_copy(obs_hbm.at[span, :], obs.at[span, :], load_sem.at[2, g]),
        )

    barrier = pltpu.get_barrier_semaphore()
    for d in (-2, -1, 1, 2):
        @pl.when(both(tm + d >= 0, tm + d < tm_size))
        def _():
            pl.semaphore_signal(barrier, inc=1, device_id=(s, tm + d), device_id_type=pl.DeviceIdType.MESH)
    for to in (following, previous):
        pl.semaphore_signal(barrier, inc=1, device_id=(to, tm), device_id_type=pl.DeviceIdType.MESH)

    x_load = pltpu.make_async_copy(x_hbm, x_in, x_sem.at[0])
    x_load.start()

    @pl.loop(0, groups)
    def _(g):
        for c in load_copies(g):
            c.start()

    x_load.wait()

    ar_rows = piece_rows(half - 1)

    def edge_copies(it, source):
        to_right = remote(
            source.at[ar_rows, pl.ds(hours - HALO, HALO)], halo_l.at[it],
            edge_send.at[it, 0], edge_recv.at[it, 0], s, tm + 1,
        )
        to_left = remote(
            source.at[ar_rows, pl.ds(0, HALO)], halo_r.at[it],
            edge_send.at[it, 1], edge_recv.at[it, 1], s, tm - 1,
        )
        return to_right, to_left

    def start_edges(it, source):
        to_right, to_left = edge_copies(it, source)
        pl.when(tm < tm_size - 1)(to_right.start)
        pl.when(tm > 0)(to_left.start)

    f_at = (f_in, f_mid, f_out)
    x_at = (x_in, x_mid, x_out)

    def pair_copy(it, g):
        return remote(
            grad.at[it, own_rows(g, 1 - core), :], partner_in.at[it, slot_group(g), :],
            pair_send.at[it], pair_recv.at[it, g], s, partner,
        )

    def send_inward(it, j):
        view = grad.at[it, line_rows(j), :]

        @pl.when(is_mid)
        def _():
            remote(view, inner_in.at[it, slot_rows(j), :], in_send.at[it], inner_recv.at[it, j], s, inward).start()

        @pl.when(jnp.logical_not(is_mid))
        def _():
            remote(view, outer_in.at[it, slot_rows(j), :], in_send.at[it], outer_recv.at[it, j], s, inward).start()

    def outward_copy(it, j):
        view = f_at[it + 1].at[line_rows(j), :]
        return remote(view, view, spread_send.at[it], inner_recv.at[it, j], s, outward)

    def give_copy(it, g, which):
        view = f_at[it + 1].at[own_rows(g, which), :]
        return remote(view, view, give_send.at[it], give_recv.at[it, g], s, partner)

    def merge(it, g):
        pair_copy(it, g).wait_recv()
        grad[it, own_rows(g, core), :] += partner_in[it, slot_group(g), :]

        @pl.when(is_end)
        def _():
            for k in range(SUBS):
                send_inward(it, g * SUBS + k)

    def line_step(it, j):
        @pl.when(both(not_end, j < blocks))
        def _():
            slot = outer_in.at[it, slot_rows(j), :]
            remote(slot, slot, in_send.at[it], outer_recv.at[it, j], s, inward).wait_recv()
            grad[it, line_rows(j), :] += outer_in[it, slot_rows(j), :]
            send_inward(it, j)

        i = j - lag

        @pl.when(both(i >= 0, i < blocks))
        def _():
            @pl.when(is_mid)
            def _():
                slot = inner_in.at[it, slot_rows(i), :]
                remote(slot, slot, in_send.at[it], inner_recv.at[it, i], s, inward).wait_recv()
                old = f_at[it][line_rows(i), :]
                total = grad[it, line_rows(i), :] + inner_in[it, slot_rows(i), :]
                f_at[it + 1][line_rows(i), :] = old - step_f * (total + ridge_f * old)

            @pl.when(jnp.logical_not(is_mid))
            def _():
                outward_copy(it, i).wait_recv()

            pl.when(not_end)(outward_copy(it, i).start)
            pl.when(i % SUBS == SUBS - 1)(give_copy(it, i // SUBS, core).start)

    line_done = [0] * ITERS

    def run_line(it, stop):
        stop = min(stop, blocks + last_lag)
        if stop > line_done[it]:
            def body(j, carry):
                line_step(it, j)
                return carry

            lax.fori_loop(line_done[it], stop, body, 0)
            line_done[it] = stop

    def row_pass(it, g):
        span = group_rows(g)
        low = f_at[it][span, :].astype(jnp.bfloat16)
        f_low[span, :] = low
        product = jnp.dot(low, x_low[...], preferred_element_type=jnp.float32)
        miss = jnp.where(
            mask[span, :] != 0,
            product - obs[span, :].astype(jnp.float32),
            jnp.zeros_like(product),
        ).astype(jnp.bfloat16)
        misfit[span, :] = miss
        grad[it, span, :] = lax.dot_general(
            miss, x_low[...], (((1,), (1,)), ((), ())), preferred_element_type=jnp.float32
        )

    def up_copy(it, p, c):
        forward = p < half
        to = p + 1 if forward else p - 1
        dst = up_in.at[it, to, :, columns(c)]
        return remote(
            g_loc.at[it, piece_rows(p), columns(c)], dst, up_send.at[it], up_recv.at[it, to, c],
            following if forward else previous, tm,
        )

    def cross_copy(it, p, c):
        forward = p < half
        side = 1 if forward else 0
        return remote(
            g_loc.at[it, piece_rows(p), columns(c)], cross_in.at[it, side, :, columns(c)],
            cross_send.at[it], cross_recv.at[it, side, c], following if forward else previous, tm,
        )

    def share_copy(it, p, c):
        forward = p < half
        to = p - 1 if forward else p + 1
        view = x_at[it + 1].at[piece_rows(p), columns(c)]
        return remote(
            view, view, share_send.at[it], share_recv.at[it, to, c], previous if forward else following, tm,
        )

    def up_wait(it, p, c):
        slot = up_in.at[it, p, :, columns(c)]
        remote(slot, slot, up_send.at[it], up_recv.at[it, p, c], following, tm).wait_recv()

    def cross_wait(it, side, c):
        slot = cross_in.at[it, side, :, columns(c)]
        remote(slot, slot, cross_send.at[it], cross_recv.at[it, side, c], following, tm).wait_recv()

    def share_wait(it, p, c):
        view = x_at[it + 1].at[piece_rows(p), columns(c)]
        remote(view, view, share_send.at[it], share_recv.at[it, p, c], following, tm).wait_recv()

    def collect(it, depth, c):
        for p in (depth, series_size - 1 - depth):
            up_wait(it, p, c)
            total = g_loc[it, piece_rows(p), columns(c)] + up_in[it, p, :, columns(c)]
            if p == half - 1:
                total = total + lam_ar * ar[:, columns(c)]
            g_loc[it, piece_rows(p), columns(c)] = total
            (cross_copy if depth == half - 1 else up_copy)(it, p, c).start()

    def update(it, c):
        for p in (half - 1, half):
            side = p // half
            cross_wait(it, side, c)
            total = g_loc[it, piece_rows(p), columns(c)] + cross_in[it, side, :, columns(c)]
            old = x_at[it][piece_rows(p), columns(c)]
            x_at[it + 1][piece_rows(p), columns(c)] = old - step_x * (total + ridge_x * old)
            share_copy(it, p, c).start()

    def share(it, depth, c):
        for p in (depth, series_size - 1 - depth):
            share_wait(it, p, c)
            if depth > 0:
                share_copy(it, p, c).start()

    def residuals(it):
        x_now = x_at[it]
        to_right, to_left = edge_copies(it, x_now)

        @pl.when(tm > 0)
        def _():
            to_right.wait_recv()

        @pl.when(tm == 0)
        def _():
            halo_l[it] = jnp.zeros_like(halo_l[it])

        @pl.when(tm < tm_size - 1)
        def _():
            to_left.wait_recv()

        @pl.when(tm == tm_size - 1)
        def _():
            halo_r[it] = jnp.zeros_like(halo_r[it])

        extended = jnp.concatenate([halo_l[it], x_now[ar_rows, :], halo_r[it]], axis=1)
        width = hours + 2 * HALO
        weights = [w_cols[lag_at, ar_rows, :][:, 0:1] for lag_at in range(3)]
        resid = extended
        for lag_at in range(3):
            resid = resid - weights[lag_at] * pltpu.roll(extended, LAGS[lag_at], 1)
        hour = lax.broadcasted_iota(jnp.int32, (piece, width), 1) + (tm * hours - HALO)
        resid = jnp.where(both(hour >= 168, hour < hours_all), resid, jnp.zeros_like(resid))
        back = None
        for lag_at in range(3):
            term = weights[lag_at] * pltpu.roll(resid, width - LAGS[lag_at], 1)
            back = term if back is None else back + term
        ar[...] = (resid - back)[:, HALO : HALO + hours]

    for it in range(ITERS):
        x_low[...] = x_at[it][...].astype(jnp.bfloat16)
        for g in range(groups):
            if it == 0:
                for c in load_copies(g):
                    c.wait()
            else:
                run_line(it - 1, (g + 1) * SUBS + last_lag)
                give_copy(it - 1, g, 1 - core).wait_recv()
            row_pass(it, g)
            if it == 0 and g == 0:
                neighbours = jnp.minimum(tm, 2) + jnp.minimum(tm_size - 1 - tm, 2)
                pl.semaphore_wait(barrier, 2 + neighbours)
                start_edges(0, x_in)
            pair_copy(it, g).start()
            if g > 0:
                merge(it, g - 1)
            if it > 0:
                run_line(it, Z_NEXT[min(g, len(Z_NEXT) - 1)])
        merge(it, groups - 1)
        for c in range(parts):
            g_loc[it, :, columns(c)] = lax.dot_general(
                f_low[...], misfit[:, columns(c)], (((0,), (0,)), ((), ())),
                preferred_element_type=jnp.float32,
            )
            for p in (0, series_size - 1):
                up_copy(it, p, c).start()
            run_line(it, Z_AT_G[it][min(c, 2)])
        if it == 0:
            for lag_at in range(3):
                w_cols[lag_at] = jnp.transpose(jnp.broadcast_to(w_in[lag_at : lag_at + 1, :], (128, rank)))
        residuals(it)
        run_line(it, Z_AT_AR[it])
        events = []
        for depth in range(1, half):
            events += [(collect, depth, c) for c in range(parts)]
        events += [(lambda it, _, c: update(it, c), 0, c) for c in range(parts)]
        for depth in range(half - 2, -1, -1):
            events += [(share, depth, c) for c in range(parts)]
        for e, (step, depth, c) in enumerate(events):
            run_line(it, Z_AT_X[it] + Z_PER_X * e)
            step(it, depth, c)
        if it < ITERS - 1:
            start_edges(it + 1, x_at[it + 1])
    run_line(ITERS - 1, blocks + last_lag)
    for g in range(groups):
        give_copy(ITERS - 1, g, 1 - core).wait_recv()

    for it in range(ITERS):
        to_right, to_left = edge_copies(it, x_at[it])
        pl.when(tm < tm_size - 1)(to_right.wait_send)
        pl.when(tm > 0)(to_left.wait_send)
        line = partner_in.at[it]
        for sem in (pair_send, in_send, give_send):
            remote(line, line, sem.at[it], pair_recv.at[it, 0], s, partner).wait_send()

        @pl.when(not_end)
        def _():
            remote(line, line, spread_send.at[it], pair_recv.at[it, 0], s, partner).wait_send()

        many = up_in.at[it, pl.ds(0, series_size - 2)]
        two = cross_in.at[it]
        for view, sem in ((many, up_send), (two, cross_send), (many, share_send)):
            remote(view, view, sem.at[it], cross_recv.at[it, 0, 0], following, tm).wait_send()


def final_product(f_ref, x_ref, f_out, x_out, imputed, x_low, low, copy_sem, out_sem):
    tall = f_ref.shape[0] // TAIL_STEPS
    copies = (
        pltpu.make_async_copy(f_ref, f_out, copy_sem.at[0]),
        pltpu.make_async_copy(x_ref, x_out, copy_sem.at[1]),
    )
    x_low[...] = x_ref[...].astype(jnp.bfloat16)
    outs = []
    for i in range(TAIL_STEPS):
        span = pl.ds(i * tall, tall)
        low[span, :] = jnp.dot(
            f_ref[span, :].astype(jnp.bfloat16), x_low[...], preferred_element_type=jnp.float32
        ).astype(jnp.bfloat16)
        outs.append(pltpu.make_async_copy(low.at[span, :], imputed.at[span, :], out_sem.at[i]))
        outs[-1].start()
        if i == 0:
            for c in copies:
                c.start()
    for c in (*copies, *outs):
        c.wait()


def solution(mesh):
    series_size, tm_size = mesh.shape["series"], mesh.shape["tm"]

    def local(observed, mask, series_factors, time_factors, ar_weights):
        rows, rank = series_factors.shape
        hours = time_factors.shape[1]
        groups = rows // GROUP
        blocks = groups * SUBS
        parts = hours // WIDTH
        piece = rank // series_size
        f32, bf16 = jnp.float32, jnp.bfloat16
        vmem = pl.BlockSpec(memory_space=pltpu.VMEM)
        hbm = pl.BlockSpec(memory_space=pltpu.HBM)
        dma = pltpu.SemaphoreType.DMA
        line = (ITERS, rows // 2, rank)
        f_last, x_last = pl.pallas_call(
            functools.partial(kernel, series_size, tm_size),
            out_shape=(pltpu.VMEM((rows, rank), f32), pltpu.VMEM((rank, hours), f32)),
            in_specs=[hbm, hbm, hbm, hbm, vmem],
            out_specs=(vmem, vmem),
            scratch_shapes=[
                pltpu.VMEM((rows, hours), bf16),
                pltpu.VMEM((rows, hours), jnp.int32),
                pltpu.VMEM((rows, rank), f32),
                pltpu.VMEM((rank, hours), f32),
                pltpu.VMEM((rows, rank), f32),
                pltpu.VMEM((rank, hours), f32),
                pltpu.VMEM((piece, hours), f32),
                pltpu.VMEM((rows, hours), bf16),
                pltpu.VMEM((rows, rank), bf16),
                pltpu.VMEM((rank, hours), bf16),
                pltpu.VMEM((ITERS, rows, rank), f32),
                pltpu.VMEM(line, f32),
                pltpu.VMEM(line, f32),
                pltpu.VMEM(line, f32),
                pltpu.VMEM((ITERS, rank, hours), f32),
                pltpu.VMEM((ITERS, series_size, piece, hours), f32),
                pltpu.VMEM((ITERS, 2, piece, hours), f32),
                pltpu.VMEM((ITERS, piece, HALO), f32),
                pltpu.VMEM((ITERS, piece, HALO), f32),
                pltpu.VMEM((3, rank, 128), f32),
                dma((3, groups)), dma((1,)),
                dma((ITERS,)), dma((ITERS,)), dma((ITERS,)), dma((ITERS,)),
                dma((ITERS,)), dma((ITERS,)), dma((ITERS,)), dma((ITERS, 2)),
                dma((ITERS, groups)), dma((ITERS, groups)),
                dma((ITERS, blocks)), dma((ITERS, blocks)),
                dma((ITERS, series_size, parts)), dma((ITERS, 2, parts)), dma((ITERS, series_size, parts)),
                dma((ITERS, 2)),
            ],
            compiler_params=pltpu.CompilerParams(
                collective_id=0, has_side_effects=True,
                vmem_limit_bytes=VMEM_BYTES - 4 * rank * (rows + hours) - VMEM_SPARE,
            ),
        )(observed, mask, series_factors, time_factors, ar_weights)
        anywhere = pl.BlockSpec(memory_space=pl.ANY)
        return tuple(pl.pallas_call(
            final_product,
            out_shape=(
                jax.ShapeDtypeStruct((rows, rank), f32),
                jax.ShapeDtypeStruct((rank, hours), f32),
                jax.ShapeDtypeStruct((rows, hours), bf16),
            ),
            in_specs=[vmem, vmem],
            out_specs=(anywhere, anywhere, anywhere),
            scratch_shapes=[
                pltpu.VMEM((rank, hours), bf16),
                pltpu.VMEM((rows, hours), bf16),
                dma((2,)),
                dma((TAIL_STEPS,)),
            ],
            compiler_params=pltpu.CompilerParams(vmem_limit_bytes=16 * 1024 * 1024),
        )(f_last, x_last))

    in_specs = (P("series", "tm"), P("series", "tm"), P("series", None), P(None, "tm"), P())
    out_specs = (P("series", None), P(None, "tm"), P("series", "tm"))
    return jax.shard_map(local, mesh=mesh, in_specs=in_specs, out_specs=out_specs, check_vma=False)
```

time: 68.3 us -> 58.4 us (0.86)
  Pallas kernels: 67.4 us -> 57.6 us
    pallas_call x1, Pallas kernels: 63.6 us -> 55.3 us  [local(): pl.pallas_call(functools.partial(kernel, series_size, tm_size), out_shape...]
    pallas_call x1, Pallas kernels: 3.78 us -> 2.29 us  [local(): pl.pallas_call(final_product, out_shape=(jax.ShapeDtypeStruct((rows, rank...]
where the time goes in v1:
time: 58.4 us; the launch traced here: 58.2 us
  Pallas kernels  57.6 us (99%)
  between operations  0.64 us (1%)
    pallas_call x1, Pallas kernels, local(): pl.pallas_call(functools.partial(kernel, series_size, tm_size), out_shape...  55.3 us
    pallas_call x1, Pallas kernels, local(): pl.pallas_call(final_product, out_shape=(jax.ShapeDtypeStruct((rows, rank...  2.29 us

profile of v1, /device:TPU:0, one launch (start us, length us, event | category | flops | bytes accessed | tf_op | source)
XLA Modules:
  0.0 58.2 jit_solution(12557166156749681366)
XLA Ops:
  0.6 55.3 %shard_map.76 = (f32[1280,256]{1,0:T(8,128)S(1)}, f32[256,768]{1,0:T(8,128)S(1)}) custom-call(bf16[1280,768]{1,0:T(8,128)(2,1)} %obs_hbm.1, s32[1280,768]{1,0:T(8,128)} %mask_hbm.1, f32[1280,256]{1,0:T(8,128)} %f_hbm.1, f32[256,768]{1,0:T(8,128)} %x_hbm.1, f32[3,256]{1,0:T(4,128)} %w_in.1), custom_call_target="tpu_custom_call" | custom-call | tf_op jit(solution)/shard_map/pallas_call | solution.py:448
  55.9 2.3 %shard_map.77 = (f32[1280,256]{1,0:T(8,128)}, f32[256,768]{1,0:T(8,128)}, bf16[1280,768]{1,0:T(8,128)(2,1)}) custom-call(f32[1280,256]{1,0:T(8,128)S(1)} %get-tuple-element.5.f_ref, f32[256,768]{1,0:T(8,128)S(1)} %get-tuple-element.6.x_ref), custom_call_target="tpu_custom_call" | custom-call | tf_op jit(solution)/shard_map/pallas_call | solution.py:488

commit v2 on v1

--- a/solution.py
+++ b/solution.py
@@ -14,24 +14,26 @@
 SUBS = 4
 WIDTH = 256
 LAG = 4
-HOP = 3
+HOP = 5
 TAIL_STEPS = 5
 VMEM_BYTES = 67043328
 VMEM_SPARE = 64 * 1024
-Z_AT_G = ((1, 2, 3), (5, 6, 7))
-Z_AT_AR = (5, 8)
-Z_AT_X = (5, 8)
+Z_FIRST = 1
+Z_AT_X = (1, 10)
 Z_PER_X = 2
-Z_NEXT = (0, 0, 0, 2, 4)
+Z_MID = (18, 19, 20, 24)
+Z_LAST = (6, 7)
+VMEM_BYTES = 67043328
+VMEM_SPARE = 64 * 1024
 
 
 def kernel(
     series_size, tm_size,
-    obs_hbm, mask_hbm, f_hbm, x_hbm, w_in,
+    obs_hbm, mask_hbm, f_hbm, x_hbm, w_hbm,
     f_out, x_out,
     obs, mask, f_in, x_in, f_mid, x_mid, ar, misfit, f_low, x_low, grad, partner_in, outer_in, inner_in,
-    g_loc, up_in, cross_in, halo_l, halo_r, w_cols,
-    load_sem, x_sem, pair_send, in_send, spread_send, give_send, up_send, cross_send, share_send, edge_send,
+    g_loc, up_in, cross_in, halo_l, halo_r, w_in, w_cols,
+    load_sem, pair_send, in_send, spread_send, give_send, up_send, cross_send, share_send, edge_send,
     pair_recv, give_recv, outer_recv, inner_recv, up_recv, cross_recv, share_recv, edge_recv,
 ):
     rows, rank = f_in.shape
@@ -112,13 +114,31 @@
     def columns(c):
         return pl.ds(c * WIDTH, WIDTH)
 
-    def load_copies(g):
-        span = group_rows(g)
+    first_rows, other_rows = pl.ds(0, GROUP), pl.ds(GROUP, rows - GROUP)
+    every_hour = pl.ds(0, hours)
+
+    def load(k, hbm, vmem, row_span, hour_span):
+        return pltpu.make_async_copy(hbm.at[row_span, hour_span], vmem.at[row_span, hour_span], load_sem.at[k])
+
+    rank_span = pl.ds(0, rank)
+    w_load = pltpu.make_async_copy(w_hbm, w_in, load_sem.at[1])
+    x_load = pltpu.make_async_copy(x_hbm, x_in, load_sem.at[0])
+    first_loads = (
+        load(2, f_hbm, f_in, first_rows, rank_span),
+        load(3, mask_hbm, mask, first_rows, every_hour),
+        load(4, obs_hbm, obs, first_rows, every_hour),
+    )
+    f_load = load(5, f_hbm, f_in, other_rows, rank_span)
+
+    def part_loads(c):
         return (
-            pltpu.make_async_copy(f_hbm.at[span, :], f_in.at[span, :], load_sem.at[0, g]),
-            pltpu.make_async_copy(mask_hbm.at[span, :], mask.at[span, :], load_sem.at[1, g]),
-            pltpu.make_async_copy(obs_hbm.at[span, :], obs.at[span, :], load_sem.at[2, g]),
-        )
+            load(6 + 2 * c, mask_hbm, mask, other_rows, columns(c)),
+            load(7 + 2 * c, obs_hbm, obs, other_rows, columns(c)),
+        )
+
+    x_load.start()
+    for load_copy in (*first_loads, f_load, *part_loads(0)):
+        load_copy.start()
 
     barrier = pltpu.get_barrier_semaphore()
     for d in (-2, -1, 1, 2):
@@ -128,15 +148,10 @@
     for to in (following, previous):
         pl.semaphore_signal(barrier, inc=1, device_id=(to, tm), device_id_type=pl.DeviceIdType.MESH)
 
-    x_load = pltpu.make_async_copy(x_hbm, x_in, x_sem.at[0])
-    x_load.start()
-
-    @pl.loop(0, groups)
-    def _(g):
-        for c in load_copies(g):
-            c.start()
-
-    x_load.wait()
+    for c in range(1, parts):
+        for load_copy in part_loads(c):
+            load_copy.start()
+    w_load.start()
 
     ar_rows = piece_rows(half - 1)
 
@@ -162,27 +177,30 @@
     def pair_copy(it, g):
         return remote(
             grad.at[it, own_rows(g, 1 - core), :], partner_in.at[it, slot_group(g), :],
-            pair_send.at[it], pair_recv.at[it, g], s, partner,
-        )
+            pair_send.at[it], pair_recv.at[g], s, partner,
+        )
+
+    def inner_slot(it, j):
+        return j + blocks * (1 - jnp.minimum(j // (LAG + 1), 1)) if it % 2 else j
 
     def send_inward(it, j):
         view = grad.at[it, line_rows(j), :]
 
         @pl.when(is_mid)
         def _():
-            remote(view, inner_in.at[it, slot_rows(j), :], in_send.at[it], inner_recv.at[it, j], s, inward).start()
+            remote(view, inner_in.at[it, slot_rows(j), :], in_send.at[it], inner_recv.at[inner_slot(it, j)], s, inward).start()
 
         @pl.when(jnp.logical_not(is_mid))
         def _():
-            remote(view, outer_in.at[it, slot_rows(j), :], in_send.at[it], outer_recv.at[it, j], s, inward).start()
+            remote(view, outer_in.at[it, slot_rows(j), :], in_send.at[it], outer_recv.at[j], s, inward).start()
 
     def outward_copy(it, j):
         view = f_at[it + 1].at[line_rows(j), :]
-        return remote(view, view, spread_send.at[it], inner_recv.at[it, j], s, outward)
+        return remote(view, view, spread_send.at[it], inner_recv.at[inner_slot(it, j)], s, outward)
 
     def give_copy(it, g, which):
         view = f_at[it + 1].at[own_rows(g, which), :]
-        return remote(view, view, give_send.at[it], give_recv.at[it, g], s, partner)
+        return remote(view, view, give_send.at[it], give_recv.at[g], s, partner)
 
     def merge(it, g):
         pair_copy(it, g).wait_recv()
@@ -197,7 +215,7 @@
         @pl.when(both(not_end, j < blocks))
         def _():
             slot = outer_in.at[it, slot_rows(j), :]
-            remote(slot, slot, in_send.at[it], outer_recv.at[it, j], s, inward).wait_recv()
+            remote(slot, slot, in_send.at[it], outer_recv.at[j], s, inward).wait_recv()
             grad[it, line_rows(j), :] += outer_in[it, slot_rows(j), :]
             send_inward(it, j)
 
@@ -208,7 +226,7 @@
             @pl.when(is_mid)
             def _():
                 slot = inner_in.at[it, slot_rows(i), :]
-                remote(slot, slot, in_send.at[it], inner_recv.at[it, i], s, inward).wait_recv()
+                remote(slot, slot, in_send.at[it], inner_recv.at[inner_slot(it, i)], s, inward).wait_recv()
                 old = f_at[it][line_rows(i), :]
                 total = grad[it, line_rows(i), :] + inner_in[it, slot_rows(i), :]
                 f_at[it + 1][line_rows(i), :] = old - step_f * (total + ridge_f * old)
@@ -221,6 +239,18 @@
             pl.when(i % SUBS == SUBS - 1)(give_copy(it, i // SUBS, core).start)
 
     line_done = [0] * ITERS
+
+    def run_both(stop):
+        stop = min(stop, blocks + last_lag)
+        start = line_done[0]
+        if stop > start:
+            def body(j, carry):
+                line_step(0, start + j)
+                line_step(1, j)
+                return carry
+
+            lax.fori_loop(0, stop - start, body, 0)
+            line_done[0], line_done[1] = stop, stop - start
 
     def run_line(it, stop):
         stop = min(stop, blocks + last_lag)
@@ -232,27 +262,66 @@
             lax.fori_loop(line_done[it], stop, body, 0)
             line_done[it] = stop
 
-    def row_pass(it, g):
-        span = group_rows(g)
-        low = f_at[it][span, :].astype(jnp.bfloat16)
-        f_low[span, :] = low
-        product = jnp.dot(low, x_low[...], preferred_element_type=jnp.float32)
-        miss = jnp.where(
-            mask[span, :] != 0,
-            product - obs[span, :].astype(jnp.float32),
-            jnp.zeros_like(product),
-        ).astype(jnp.bfloat16)
-        misfit[span, :] = miss
-        grad[it, span, :] = lax.dot_general(
-            miss, x_low[...], (((1,), (1,)), ((), ())), preferred_element_type=jnp.float32
-        )
+    def products(it, which):
+        for g in which:
+            span = group_rows(g)
+            low = f_at[it][span, :].astype(jnp.bfloat16)
+            f_low[span, :] = low
+            product = jnp.dot(low, x_low[...], preferred_element_type=jnp.float32)
+            misfit[span, :] = jnp.where(
+                mask[span, :] != 0,
+                product - obs[span, :].astype(jnp.float32),
+                jnp.zeros_like(product),
+            ).astype(jnp.bfloat16)
+
+    def products_part(which, c):
+        for g in which:
+            span = group_rows(g)
+            if c == 0:
+                f_low[span, :] = f_in[span, :].astype(jnp.bfloat16)
+            product = jnp.dot(f_low[span, :], x_low[:, columns(c)], preferred_element_type=jnp.float32)
+            misfit[span, columns(c)] = jnp.where(
+                mask[span, columns(c)] != 0,
+                product - obs[span, columns(c)].astype(jnp.float32),
+                jnp.zeros_like(product),
+            ).astype(jnp.bfloat16)
+
+    def series_grads(it, which):
+        for g in which:
+            span = group_rows(g)
+            grad[it, span, :] = lax.dot_general(
+                misfit[span, :], x_low[...], (((1,), (1,)), ((), ())), preferred_element_type=jnp.float32
+            )
+
+    def hour_grads(it, which):
+        for g in which:
+            span = group_rows(g)
+            term = lax.dot_general(
+                f_low[span, :], misfit[span, :], (((0,), (0,)), ((), ())), preferred_element_type=jnp.float32
+            )
+            if g > 0:
+                term = g_loc[it] + term
+            g_loc[it] = term
+
+    def hour_grads_part(it, c):
+        g_loc[it, :, columns(c)] = lax.dot_general(
+            f_low[...], misfit[:, columns(c)], (((0,), (0,)), ((), ())), preferred_element_type=jnp.float32
+        )
+
+    def start_pairs(it, which):
+        for g in which:
+            pair_copy(it, g).start()
+
+    def start_up(it, c):
+        for p in (0, series_size - 1):
+            up_copy(it, p, c).start()
 
     def up_copy(it, p, c):
         forward = p < half
         to = p + 1 if forward else p - 1
         dst = up_in.at[it, to, :, columns(c)]
         return remote(
-            g_loc.at[it, piece_rows(p), columns(c)], dst, up_send.at[it], up_recv.at[it, to, c],
+            g_loc.at[it, piece_rows(p), columns(c)], dst, up_send.at[it], up_recv.at[to - 1, c],
             following if forward else previous, tm,
         )
 
@@ -261,28 +330,31 @@
         side = 1 if forward else 0
         return remote(
             g_loc.at[it, piece_rows(p), columns(c)], cross_in.at[it, side, :, columns(c)],
-            cross_send.at[it], cross_recv.at[it, side, c], following if forward else previous, tm,
-        )
+            cross_send.at[it], cross_recv.at[side, c], following if forward else previous, tm,
+        )
+
+    def share_slot(p):
+        return p if p < half else p - 2
 
     def share_copy(it, p, c):
         forward = p < half
         to = p - 1 if forward else p + 1
         view = x_at[it + 1].at[piece_rows(p), columns(c)]
         return remote(
-            view, view, share_send.at[it], share_recv.at[it, to, c], previous if forward else following, tm,
+            view, view, share_send.at[it], share_recv.at[share_slot(to), c], previous if forward else following, tm,
         )
 
     def up_wait(it, p, c):
         slot = up_in.at[it, p, :, columns(c)]
-        remote(slot, slot, up_send.at[it], up_recv.at[it, p, c], following, tm).wait_recv()
+        remote(slot, slot, up_send.at[it], up_recv.at[p - 1, c], following, tm).wait_recv()
 
     def cross_wait(it, side, c):
         slot = cross_in.at[it, side, :, columns(c)]
-        remote(slot, slot, cross_send.at[it], cross_recv.at[it, side, c], following, tm).wait_recv()
+        remote(slot, slot, cross_send.at[it], cross_recv.at[side, c], following, tm).wait_recv()
 
     def share_wait(it, p, c):
         view = x_at[it + 1].at[piece_rows(p), columns(c)]
-        remote(view, view, share_send.at[it], share_recv.at[it, p, c], following, tm).wait_recv()
+        remote(view, view, share_send.at[it], share_recv.at[share_slot(p), c], following, tm).wait_recv()
 
     def collect(it, depth, c):
         for p in (depth, series_size - 1 - depth):
@@ -342,39 +414,9 @@
             back = term if back is None else back + term
         ar[...] = (resid - back)[:, HALO : HALO + hours]
 
-    for it in range(ITERS):
-        x_low[...] = x_at[it][...].astype(jnp.bfloat16)
-        for g in range(groups):
-            if it == 0:
-                for c in load_copies(g):
-                    c.wait()
-            else:
-                run_line(it - 1, (g + 1) * SUBS + last_lag)
-                give_copy(it - 1, g, 1 - core).wait_recv()
-            row_pass(it, g)
-            if it == 0 and g == 0:
-                neighbours = jnp.minimum(tm, 2) + jnp.minimum(tm_size - 1 - tm, 2)
-                pl.semaphore_wait(barrier, 2 + neighbours)
-                start_edges(0, x_in)
-            pair_copy(it, g).start()
-            if g > 0:
-                merge(it, g - 1)
-            if it > 0:
-                run_line(it, Z_NEXT[min(g, len(Z_NEXT) - 1)])
-        merge(it, groups - 1)
-        for c in range(parts):
-            g_loc[it, :, columns(c)] = lax.dot_general(
-                f_low[...], misfit[:, columns(c)], (((0,), (0,)), ((), ())),
-                preferred_element_type=jnp.float32,
-            )
-            for p in (0, series_size - 1):
-                up_copy(it, p, c).start()
-            run_line(it, Z_AT_G[it][min(c, 2)])
-        if it == 0:
-            for lag_at in range(3):
-                w_cols[lag_at] = jnp.transpose(jnp.broadcast_to(w_in[lag_at : lag_at + 1, :], (128, rank)))
-        residuals(it)
-        run_line(it, Z_AT_AR[it])
+    ns = jax.named_scope
+
+    def x_events(it):
         events = []
         for depth in range(1, half):
             events += [(collect, depth, c) for c in range(parts)]
@@ -382,13 +424,120 @@
         for depth in range(half - 2, -1, -1):
             events += [(share, depth, c) for c in range(parts)]
         for e, (step, depth, c) in enumerate(events):
-            run_line(it, Z_AT_X[it] + Z_PER_X * e)
-            step(it, depth, c)
-        if it < ITERS - 1:
-            start_edges(it + 1, x_at[it + 1])
-    run_line(ITERS - 1, blocks + last_lag)
-    for g in range(groups):
-        give_copy(ITERS - 1, g, 1 - core).wait_recv()
+            with ns(f"zx{it}_{e}"):
+                run_line(it, Z_AT_X[it] + Z_PER_X * e)
+            with ns(f"x{it}_{e}"):
+                step(it, depth, c)
+
+    every = tuple(range(groups))
+    body_groups, next_last, last = every[1:-2], every[-2], every[-1]
+
+    with ns("xload"):
+        x_load.wait()
+    x_low[...] = x_in[...].astype(jnp.bfloat16)
+    with ns("load0"):
+        for load_copy in first_loads:
+            load_copy.wait()
+    with ns("p0_0"):
+        products(0, every[:1])
+        series_grads(0, every[:1])
+    with ns("barrier"):
+        neighbours = jnp.minimum(tm, 2) + jnp.minimum(tm_size - 1 - tm, 2)
+        pl.semaphore_wait(barrier, 2 + neighbours)
+    start_pairs(0, every[:1])
+    start_edges(0, x_in)
+    with ns("load1"):
+        f_load.wait()
+    for c in range(parts):
+        with ns(f"load2_{c}"):
+            for load_copy in part_loads(c):
+                load_copy.wait()
+        with ns(f"p0_{c + 1}"):
+            products_part(every[1:], c)
+        if c == parts - 1:
+            with ns("f0_1"):
+                series_grads(0, every[1:2])
+            start_pairs(0, every[1:2])
+        with ns(f"g0_{c}"):
+            hour_grads_part(0, c)
+        start_up(0, c)
+        if c == 0:
+            with ns("m0_0"):
+                merge(0, 0)
+    with ns("f0_r"):
+        series_grads(0, every[2:])
+    start_pairs(0, every[2:])
+    with ns("m0_1"):
+        merge(0, 1)
+    with ns("ar0"):
+        w_load.wait()
+        for lag_at in range(3):
+            w_cols[lag_at] = jnp.transpose(jnp.broadcast_to(w_in[lag_at : lag_at + 1, :], (128, rank)))
+        residuals(0)
+    with ns("z0_a"):
+        run_line(0, Z_FIRST)
+    with ns("m0_r"):
+        for g in every[2:]:
+            merge(0, g)
+    x_events(0)
+    start_edges(1, x_mid)
+
+    x_low[...] = x_mid[...].astype(jnp.bfloat16)
+    def take(g):
+        run_line(0, (g + 1) * SUBS + last_lag)
+        give_copy(0, g, 1 - core).wait_recv()
+
+    for g in every[:-2]:
+        with ns(f"t1_{g}"):
+            take(g)
+        with ns(f"p1_{g}"):
+            products(1, (g,))
+            series_grads(1, (g,))
+        start_pairs(1, (g,))
+        with ns(f"zm1_{g}"):
+            run_line(0, Z_MID[min(g, len(Z_MID) - 1)])
+        if g > 0:
+            with ns(f"m1_{g - 1}"):
+                merge(1, g - 1)
+    with ns("g1_a"):
+        hour_grads(1, every[:-2])
+    with ns("t1_c"):
+        run_line(0, Z_MID[-1])
+        take(next_last)
+    with ns("ar1"):
+        residuals(1)
+    with ns("p1_c"):
+        products(1, (next_last,))
+        series_grads(1, (next_last,))
+    start_pairs(1, (next_last,))
+    with ns("m1_b"):
+        merge(1, next_last - 1)
+    with ns("t1_d"):
+        run_both((last + 1) * SUBS + last_lag)
+        take(last)
+    with ns("p1_d"):
+        products(1, (last,))
+        hour_grads(1, (next_last, last))
+    for c in range(parts):
+        start_up(1, c)
+    with ns("z1_a"):
+        run_line(1, Z_LAST[0])
+    with ns("f1_d"):
+        series_grads(1, (last,))
+    start_pairs(1, (last,))
+    with ns("m1_c"):
+        merge(1, next_last)
+    with ns("z1_b"):
+        run_line(1, Z_LAST[1])
+    with ns("m1_d"):
+        merge(1, last)
+    x_events(1)
+    with ns("zend"):
+        run_line(1, blocks + last_lag)
+    with ns("gend"):
+        for g in every:
+            give_copy(1, g, 1 - core).wait_recv()
+    sc = ns("drain"); sc.__enter__()
 
     for it in range(ITERS):
         to_right, to_left = edge_copies(it, x_at[it])
@@ -396,16 +545,17 @@
         pl.when(tm > 0)(to_left.wait_send)
         line = partner_in.at[it]
         for sem in (pair_send, in_send, give_send):
-            remote(line, line, sem.at[it], pair_recv.at[it, 0], s, partner).wait_send()
+            remote(line, line, sem.at[it], pair_recv.at[0], s, partner).wait_send()
 
         @pl.when(not_end)
         def _():
-            remote(line, line, spread_send.at[it], pair_recv.at[it, 0], s, partner).wait_send()
+            remote(line, line, spread_send.at[it], pair_recv.at[0], s, partner).wait_send()
 
         many = up_in.at[it, pl.ds(0, series_size - 2)]
         two = cross_in.at[it]
         for view, sem in ((many, up_send), (two, cross_send), (many, share_send)):
-            remote(view, view, sem.at[it], cross_recv.at[it, 0, 0], following, tm).wait_send()
+            remote(view, view, sem.at[it], cross_recv.at[0, 0], following, tm).wait_send()
+    sc.__exit__(None, None, None)
 
 
 def final_product(f_ref, x_ref, f_out, x_out, imputed, x_low, low, copy_sem, out_sem):
@@ -448,7 +598,7 @@
         f_last, x_last = pl.pallas_call(
             functools.partial(kernel, series_size, tm_size),
             out_shape=(pltpu.VMEM((rows, rank), f32), pltpu.VMEM((rank, hours), f32)),
-            in_specs=[hbm, hbm, hbm, hbm, vmem],
+            in_specs=[hbm] * 5,
             out_specs=(vmem, vmem),
             scratch_shapes=[
                 pltpu.VMEM((rows, hours), bf16),
@@ -470,13 +620,14 @@
                 pltpu.VMEM((ITERS, 2, piece, hours), f32),
                 pltpu.VMEM((ITERS, piece, HALO), f32),
                 pltpu.VMEM((ITERS, piece, HALO), f32),
+                pltpu.VMEM((3, rank), f32),
                 pltpu.VMEM((3, rank, 128), f32),
-                dma((3, groups)), dma((1,)),
+                dma((6 + 2 * parts,)),
                 dma((ITERS,)), dma((ITERS,)), dma((ITERS,)), dma((ITERS,)),
                 dma((ITERS,)), dma((ITERS,)), dma((ITERS,)), dma((ITERS, 2)),
-                dma((ITERS, groups)), dma((ITERS, groups)),
-                dma((ITERS, blocks)), dma((ITERS, blocks)),
-                dma((ITERS, series_size, parts)), dma((ITERS, 2, parts)), dma((ITERS, series_size, parts)),
+                dma((groups,)), dma((groups,)),
+                dma((blocks,)), dma((blocks + LAG + 1,)),
+                dma((series_size - 2, parts)), dma((2, parts)), dma((series_size - 2, parts)),
                 dma((ITERS, 2)),
             ],
             compiler_params=pltpu.CompilerParams(

time: 58.4 us -> 51.4 us (0.88)
  Pallas kernels: 57.6 us -> 50.6 us
    pallas_call x1, Pallas kernels: 55.3 us -> 48.3 us  [local(): pl.pallas_call(functools.partial(kernel, series_size, tm_size), out_shape...]
where the time goes in v2:
time: 51.4 us; the launch traced here: 51.2 us
  Pallas kernels  50.6 us (98%)
  between operations  0.64 us (1%)
    pallas_call x1, Pallas kernels, local(): pl.pallas_call(functools.partial(kernel, series_size, tm_size), out_shape...  48.3 us
    pallas_call x1, Pallas kernels, local(): pl.pallas_call(final_product, out_shape=(jax.ShapeDtypeStruct((rows, rank...  2.29 us

profile of v2, /device:TPU:0, one launch (start us, length us, event | category | flops | bytes accessed | tf_op | source)
XLA Modules:
  0.0 51.2 jit_solution(6595335694529655705)
XLA Ops:
  0.6 48.3 %shard_map.76 = (f32[1280,256]{1,0:T(8,128)S(1)}, f32[256,768]{1,0:T(8,128)S(1)}) custom-call(bf16[1280,768]{1,0:T(8,128)(2,1)} %obs_hbm.1, s32[1280,768]{1,0:T(8,128)} %mask_hbm.1, f32[1280,256]{1,0:T(8,128)} %f_hbm.1, f32[256,768]{1,0:T(8,128)} %x_hbm.1, f32[3,256]{1,0:T(4,128)} %w_hbm.1), custom_call_target="tpu_custom_call" | custom-call | tf_op jit(solution)/shard_map/pallas_call | solution.py:598
  49.0 2.3 %shard_map.77 = (f32[1280,256]{1,0:T(8,128)}, f32[256,768]{1,0:T(8,128)}, bf16[1280,768]{1,0:T(8,128)(2,1)}) custom-call(f32[1280,256]{1,0:T(8,128)S(1)} %get-tuple-element.5.f_ref, f32[256,768]{1,0:T(8,128)S(1)} %get-tuple-element.6.x_ref), custom_call_target="tpu_custom_call" | custom-call | tf_op jit(solution)/shard_map/pallas_call | solution.py:639

commit v3 on v2

--- a/solution.py
+++ b/solution.py
@@ -15,14 +15,15 @@
 WIDTH = 256
 LAG = 4
 HOP = 5
-TAIL_STEPS = 5
+TALL = 512
 VMEM_BYTES = 67043328
 VMEM_SPARE = 64 * 1024
 Z_FIRST = 1
-Z_AT_X = (1, 10)
+Z_AT_X = (1, 14)
 Z_PER_X = 2
 Z_MID = (18, 19, 20, 24)
-Z_LAST = (6, 7)
+Z_NEXT = 1
+Z_LAST = (6, 7, 8)
 VMEM_BYTES = 67043328
 VMEM_SPARE = 64 * 1024
 
@@ -33,7 +34,7 @@
     f_out, x_out,
     obs, mask, f_in, x_in, f_mid, x_mid, ar, misfit, f_low, x_low, grad, partner_in, outer_in, inner_in,
     g_loc, up_in, cross_in, halo_l, halo_r, w_in, w_cols,
-    load_sem, pair_send, in_send, spread_send, give_send, up_send, cross_send, share_send, edge_send,
+    load_sem,
     pair_recv, give_recv, outer_recv, inner_recv, up_recv, cross_recv, share_recv, edge_recv,
 ):
     rows, rank = f_in.shape
@@ -52,6 +53,9 @@
     ridge_x = 0.1 * sensors_all
     lam_ar = sensors_all / 8.0
 
+    pair_send, right_send, left_send, in_send, up_send, give_send, spread_send, cross_send, share_send = (
+        load_sem.at[k] for k in (0, 2, 3, 4, 5, 6, 7, 8, 9)
+    )
     s = lax.axis_index("series")
     tm = lax.axis_index("tm")
     core = tm % 2
@@ -158,18 +162,26 @@
     def edge_copies(it, source):
         to_right = remote(
             source.at[ar_rows, pl.ds(hours - HALO, HALO)], halo_l.at[it],
-            edge_send.at[it, 0], edge_recv.at[it, 0], s, tm + 1,
+            right_send, edge_recv.at[it, 0], s, tm + 1,
         )
         to_left = remote(
             source.at[ar_rows, pl.ds(0, HALO)], halo_r.at[it],
-            edge_send.at[it, 1], edge_recv.at[it, 1], s, tm - 1,
+            left_send, edge_recv.at[it, 1], s, tm - 1,
         )
         return to_right, to_left
+
+    right_out = both(right == 1, core == 1)
+    left_out = both(right == 0, core == 0)
 
     def start_edges(it, source):
         to_right, to_left = edge_copies(it, source)
-        pl.when(tm < tm_size - 1)(to_right.start)
-        pl.when(tm > 0)(to_left.start)
+        pl.when(both(tm < tm_size - 1, jnp.logical_not(right_out)))(to_right.start)
+        pl.when(both(tm > 0, jnp.logical_not(left_out)))(to_left.start)
+
+    def start_outward_edges(it, source):
+        to_right, to_left = edge_copies(it, source)
+        pl.when(both(tm < tm_size - 1, right_out))(to_right.start)
+        pl.when(both(tm > 0, left_out))(to_left.start)
 
     f_at = (f_in, f_mid, f_out)
     x_at = (x_in, x_mid, x_out)
@@ -177,7 +189,7 @@
     def pair_copy(it, g):
         return remote(
             grad.at[it, own_rows(g, 1 - core), :], partner_in.at[it, slot_group(g), :],
-            pair_send.at[it], pair_recv.at[g], s, partner,
+            pair_send, pair_recv.at[g], s, partner,
         )
 
     def inner_slot(it, j):
@@ -188,19 +200,19 @@
 
         @pl.when(is_mid)
         def _():
-            remote(view, inner_in.at[it, slot_rows(j), :], in_send.at[it], inner_recv.at[inner_slot(it, j)], s, inward).start()
+            remote(view, inner_in.at[it, slot_rows(j), :], in_send, inner_recv.at[inner_slot(it, j)], s, inward).start()
 
         @pl.when(jnp.logical_not(is_mid))
         def _():
-            remote(view, outer_in.at[it, slot_rows(j), :], in_send.at[it], outer_recv.at[j], s, inward).start()
+            remote(view, outer_in.at[it, slot_rows(j), :], in_send, outer_recv.at[j], s, inward).start()
 
     def outward_copy(it, j):
         view = f_at[it + 1].at[line_rows(j), :]
-        return remote(view, view, spread_send.at[it], inner_recv.at[inner_slot(it, j)], s, outward)
+        return remote(view, view, spread_send, inner_recv.at[inner_slot(it, j)], s, outward)
 
     def give_copy(it, g, which):
         view = f_at[it + 1].at[own_rows(g, which), :]
-        return remote(view, view, give_send.at[it], give_recv.at[g], s, partner)
+        return remote(view, view, give_send, give_recv.at[g], s, partner)
 
     def merge(it, g):
         pair_copy(it, g).wait_recv()
@@ -215,7 +227,7 @@
         @pl.when(both(not_end, j < blocks))
         def _():
             slot = outer_in.at[it, slot_rows(j), :]
-            remote(slot, slot, in_send.at[it], outer_recv.at[j], s, inward).wait_recv()
+            remote(slot, slot, in_send, outer_recv.at[j], s, inward).wait_recv()
             grad[it, line_rows(j), :] += outer_in[it, slot_rows(j), :]
             send_inward(it, j)
 
@@ -226,7 +238,7 @@
             @pl.when(is_mid)
             def _():
                 slot = inner_in.at[it, slot_rows(i), :]
-                remote(slot, slot, in_send.at[it], inner_recv.at[inner_slot(it, i)], s, inward).wait_recv()
+                remote(slot, slot, in_send, inner_recv.at[inner_slot(it, i)], s, inward).wait_recv()
                 old = f_at[it][line_rows(i), :]
                 total = grad[it, line_rows(i), :] + inner_in[it, slot_rows(i), :]
                 f_at[it + 1][line_rows(i), :] = old - step_f * (total + ridge_f * old)
@@ -246,11 +258,12 @@
         if stop > start:
             def body(j, carry):
                 line_step(0, start + j)
-                line_step(1, j)
+                line_step(1, begun + j)
                 return carry
 
+            begun = line_done[1]
             lax.fori_loop(0, stop - start, body, 0)
-            line_done[0], line_done[1] = stop, stop - start
+            line_done[0], line_done[1] = stop, begun + stop - start
 
     def run_line(it, stop):
         stop = min(stop, blocks + last_lag)
@@ -303,6 +316,12 @@
                 term = g_loc[it] + term
             g_loc[it] = term
 
+    def hour_grads_add(g, c):
+        span = group_rows(g)
+        g_loc[1, :, columns(c)] += lax.dot_general(
+            f_low[span, :], misfit[span, columns(c)], (((0,), (0,)), ((), ())), preferred_element_type=jnp.float32
+        )
+
     def hour_grads_part(it, c):
         g_loc[it, :, columns(c)] = lax.dot_general(
             f_low[...], misfit[:, columns(c)], (((0,), (0,)), ((), ())), preferred_element_type=jnp.float32
@@ -321,7 +340,7 @@
         to = p + 1 if forward else p - 1
         dst = up_in.at[it, to, :, columns(c)]
         return remote(
-            g_loc.at[it, piece_rows(p), columns(c)], dst, up_send.at[it], up_recv.at[to - 1, c],
+            g_loc.at[it, piece_rows(p), columns(c)], dst, up_send, up_recv.at[to - 1, c],
             following if forward else previous, tm,
         )
 
@@ -330,7 +349,7 @@
         side = 1 if forward else 0
         return remote(
             g_loc.at[it, piece_rows(p), columns(c)], cross_in.at[it, side, :, columns(c)],
-            cross_send.at[it], cross_recv.at[side, c], following if forward else previous, tm,
+            cross_send, cross_recv.at[side, c], following if forward else previous, tm,
         )
 
     def share_slot(p):
@@ -341,20 +360,20 @@
         to = p - 1 if forward else p + 1
         view = x_at[it + 1].at[piece_rows(p), columns(c)]
         return remote(
-            view, view, share_send.at[it], share_recv.at[share_slot(to), c], previous if forward else following, tm,
+            view, view, share_send, share_recv.at[share_slot(to), c], previous if forward else following, tm,
         )
 
     def up_wait(it, p, c):
         slot = up_in.at[it, p, :, columns(c)]
-        remote(slot, slot, up_send.at[it], up_recv.at[p - 1, c], following, tm).wait_recv()
+        remote(slot, slot, up_send, up_recv.at[p - 1, c], following, tm).wait_recv()
 
     def cross_wait(it, side, c):
         slot = cross_in.at[it, side, :, columns(c)]
-        remote(slot, slot, cross_send.at[it], cross_recv.at[side, c], following, tm).wait_recv()
+        remote(slot, slot, cross_send, cross_recv.at[side, c], following, tm).wait_recv()
 
     def share_wait(it, p, c):
         view = x_at[it + 1].at[piece_rows(p), columns(c)]
-        remote(view, view, share_send.at[it], share_recv.at[share_slot(p), c], following, tm).wait_recv()
+        remote(view, view, share_send, share_recv.at[share_slot(p), c], following, tm).wait_recv()
 
     def collect(it, depth, c):
         for p in (depth, series_size - 1 - depth):
@@ -428,6 +447,8 @@
                 run_line(it, Z_AT_X[it] + Z_PER_X * e)
             with ns(f"x{it}_{e}"):
                 step(it, depth, c)
+            if it > 0 and e == 0:
+                pl.when(not_end)(lambda: merge(1, last))
 
     every = tuple(range(groups))
     body_groups, next_last, last = every[1:-2], every[-2], every[-1]
@@ -446,6 +467,7 @@
         pl.semaphore_wait(barrier, 2 + neighbours)
     start_pairs(0, every[:1])
     start_edges(0, x_in)
+    start_outward_edges(0, x_in)
     with ns("load1"):
         f_load.wait()
     for c in range(parts):
@@ -504,11 +526,13 @@
     with ns("t1_c"):
         run_line(0, Z_MID[-1])
         take(next_last)
-    with ns("ar1"):
-        residuals(1)
+    start_outward_edges(1, x_mid)
+    with ns("z1_1"):
+        run_line(1, Z_NEXT)
     with ns("p1_c"):
         products(1, (next_last,))
         series_grads(1, (next_last,))
+        hour_grads(1, (next_last,))
     start_pairs(1, (next_last,))
     with ns("m1_b"):
         merge(1, next_last - 1)
@@ -517,8 +541,12 @@
         take(last)
     with ns("p1_d"):
         products(1, (last,))
-        hour_grads(1, (next_last, last))
-    for c in range(parts):
+        hour_grads_add(last, 0)
+    start_up(1, 0)
+    with ns("p1_e"):
+        for c in range(1, parts):
+            hour_grads_add(last, c)
+    for c in range(1, parts):
         start_up(1, c)
     with ns("z1_a"):
         run_line(1, Z_LAST[0])
@@ -529,8 +557,12 @@
         merge(1, next_last)
     with ns("z1_b"):
         run_line(1, Z_LAST[1])
+    with ns("ar1"):
+        residuals(1)
+    with ns("z1_c"):
+        run_line(1, Z_LAST[2])
     with ns("m1_d"):
-        merge(1, last)
+        pl.when(is_end)(lambda: merge(1, last))
     x_events(1)
     with ns("zend"):
         run_line(1, blocks + last_lag)
@@ -539,44 +571,38 @@
             give_copy(1, g, 1 - core).wait_recv()
     sc = ns("drain"); sc.__enter__()
 
-    for it in range(ITERS):
-        to_right, to_left = edge_copies(it, x_at[it])
-        pl.when(tm < tm_size - 1)(to_right.wait_send)
-        pl.when(tm > 0)(to_left.wait_send)
-        line = partner_in.at[it]
-        for sem in (pair_send, in_send, give_send):
-            remote(line, line, sem.at[it], pair_recv.at[0], s, partner).wait_send()
-
-        @pl.when(not_end)
-        def _():
-            remote(line, line, spread_send.at[it], pair_recv.at[0], s, partner).wait_send()
-
-        many = up_in.at[it, pl.ds(0, series_size - 2)]
-        two = cross_in.at[it]
-        for view, sem in ((many, up_send), (two, cross_send), (many, share_send)):
-            remote(view, view, sem.at[it], cross_recv.at[0, 0], following, tm).wait_send()
+    def sent(view, sem):
+        remote(view, view, sem, cross_recv.at[0, 0], following, tm).wait_send()
+
+    pl.when(tm < tm_size - 1)(lambda: sent(halo_l, right_send))
+    pl.when(tm > 0)(lambda: sent(halo_r, left_send))
+    for sem in (pair_send, in_send, give_send):
+        sent(grad.at[0], sem)
+    pl.when(not_end)(lambda: sent(grad.at[0], spread_send))
+    many = up_in.at[:, pl.ds(0, series_size - 2)]
+    sent(many, up_send)
+    sent(many, share_send)
+    sent(cross_in, cross_send)
     sc.__exit__(None, None, None)
 
 
 def final_product(f_ref, x_ref, f_out, x_out, imputed, x_low, low, copy_sem, out_sem):
-    tall = f_ref.shape[0] // TAIL_STEPS
-    copies = (
+    rows = f_ref.shape[0]
+    copies = [
         pltpu.make_async_copy(f_ref, f_out, copy_sem.at[0]),
         pltpu.make_async_copy(x_ref, x_out, copy_sem.at[1]),
-    )
+    ]
+    for c in copies:
+        c.start()
     x_low[...] = x_ref[...].astype(jnp.bfloat16)
-    outs = []
-    for i in range(TAIL_STEPS):
-        span = pl.ds(i * tall, tall)
+    for i in range(pl.cdiv(rows, TALL)):
+        span = pl.ds(i * TALL, min(TALL, rows - i * TALL))
         low[span, :] = jnp.dot(
             f_ref[span, :].astype(jnp.bfloat16), x_low[...], preferred_element_type=jnp.float32
         ).astype(jnp.bfloat16)
-        outs.append(pltpu.make_async_copy(low.at[span, :], imputed.at[span, :], out_sem.at[i]))
-        outs[-1].start()
-        if i == 0:
-            for c in copies:
-                c.start()
-    for c in (*copies, *outs):
+        copies.append(pltpu.make_async_copy(low.at[span, :], imputed.at[span, :], out_sem.at[i]))
+        copies[-1].start()
+    for c in copies:
         c.wait()
 
 
@@ -623,8 +649,6 @@
                 pltpu.VMEM((3, rank), f32),
                 pltpu.VMEM((3, rank, 128), f32),
                 dma((6 + 2 * parts,)),
-                dma((ITERS,)), dma((ITERS,)), dma((ITERS,)), dma((ITERS,)),
-                dma((ITERS,)), dma((ITERS,)), dma((ITERS,)), dma((ITERS, 2)),
                 dma((groups,)), dma((groups,)),
                 dma((blocks,)), dma((blocks + LAG + 1,)),
                 dma((series_size - 2, parts)), dma((2, parts)), dma((series_size - 2, parts)),
@@ -649,7 +673,7 @@
                 pltpu.VMEM((rank, hours), bf16),
                 pltpu.VMEM((rows, hours), bf16),
                 dma((2,)),
-                dma((TAIL_STEPS,)),
+                dma((pl.cdiv(rows, TALL),)),
             ],
             compiler_params=pltpu.CompilerParams(vmem_limit_bytes=16 * 1024 * 1024),
         )(f_last, x_last))

time: 51.4 us -> 50.1 us (0.975)
  Pallas kernels: 50.6 us -> 49.4 us
    pallas_call x1, Pallas kernels: 48.3 us -> 47.4 us  [local(): pl.pallas_call(functools.partial(kernel, series_size, tm_size), out_shape...]
where the time goes in v3:
time: 50.1 us; the launch traced here: 50 us
  Pallas kernels  49.4 us (99%)
  between operations  0.64 us (1%)
    pallas_call x1, Pallas kernels, local(): pl.pallas_call(functools.partial(kernel, series_size, tm_size), out_shape...  47.4 us
    pallas_call x1, Pallas kernels, local(): pl.pallas_call(final_product, out_shape=(jax.ShapeDtypeStruct((rows, rank...  2 us

profile of v3, /device:TPU:0, one launch (start us, length us, event | category | flops | bytes accessed | tf_op | source)
XLA Modules:
  0.0 50.0 jit_solution(5074070631382788141)
XLA Ops:
  0.6 47.4 %shard_map.76 = (f32[1280,256]{1,0:T(8,128)S(1)}, f32[256,768]{1,0:T(8,128)S(1)}) custom-call(bf16[1280,768]{1,0:T(8,128)(2,1)} %obs_hbm.1, s32[1280,768]{1,0:T(8,128)} %mask_hbm.1, f32[1280,256]{1,0:T(8,128)} %f_hbm.1, f32[256,768]{1,0:T(8,128)} %x_hbm.1, f32[3,256]{1,0:T(4,128)} %w_hbm.1), custom_call_target="tpu_custom_call" | custom-call | tf_op jit(solution)/shard_map/pallas_call | solution.py:624
  48.0 2.0 %shard_map.77 = (f32[1280,256]{1,0:T(8,128)}, f32[256,768]{1,0:T(8,128)}, bf16[1280,768]{1,0:T(8,128)(2,1)}) custom-call(f32[1280,256]{1,0:T(8,128)S(1)} %get-tuple-element.5.f_ref, f32[256,768]{1,0:T(8,128)S(1)} %get-tuple-element.6.x_ref), custom_call_target="tpu_custom_call" | custom-call | tf_op jit(solution)/shard_map/pallas_call | solution.py:663
